TPU v7x, 512 devices: a whole 4x4x16 slice. The times are simulated.
512 devices in a mesh: row: 32 (over z, core), col: 16 (over y, x).
Axes of the slice: x: 4, y: 4, z: 16, core: 2. Of those that a mesh axis runs over, the one named last changes fastest.
Arguments:
- weights: bfloat16 [2, 24576, 6144], P(None, 'row', 'col'), may hold values from -0.15625 to 0.15625
- pattern: int32 [2, 192, 48], P(None, 'row', 'col'), may hold values 0 or 1
- sketch: bfloat16 [6144, 512], P('col'), may hold values from -6 to 6
Outputs:
- basis: float32 [2, 24576, 512], P(None, ('row', 'col'))
Inputs may be any that keep to these rules, and one draw needn't show every extreme that they name: `pattern`: 1 marks a block of the sparse part, 0 a block of the residual.
All inputs are finite; a program needn't handle non-finite values.
Results may differ from a plain program's by a relative error of at most 0.0003.
Values sent between devices are 32-bit elements; how exact they have to be, the bound alone decides.
No kernel may reach another device: no remote copies, remote signals or barrier semaphores. Data moves between devices by JAX's collectives and lax.ppermute only.
A program may use at most 64 MiB of HBM per device.

v0:
```python
import jax
import jax.numpy as jnp
from jax import lax
from jax.sharding import PartitionSpec as P

M = 24576
BLOCK = 128
LAYERS = 2


def make_basis(rows_here, gram):
    lower = jnp.linalg.cholesky(gram)
    solved = lax.linalg.triangular_solve(
        lower, rows_here, left_side=False, lower=True, transpose_a=True
    )
    return solved * jnp.sqrt(jnp.float32(M))


def local_gram(rows_here):
    return lax.dot_general(
        rows_here,
        rows_here,
        (((0,), (0,)), ((), ())),
        precision=lax.Precision.HIGHEST,
        preferred_element_type=jnp.float32,
    )


def body(weights, pattern, sketch):
    row_count = weights.shape[1]
    col_count = weights.shape[2]
    outputs = []
    for layer in range(LAYERS):
        keep = (1 - pattern[layer]).astype(jnp.bfloat16)
        shaped = (
            weights[layer].reshape(row_count // BLOCK, BLOCK, col_count // BLOCK, BLOCK)
            * keep[:, None, :, None]
        )
        leftover = shaped.reshape(row_count, col_count)
        rows_here = lax.psum_scatter(
            jnp.dot(leftover, sketch, preferred_element_type=jnp.float32),
            "col",
            scatter_dimension=0,
            tiled=True,
        )
        sampled = lax.all_gather(rows_here, "col", axis=0, tiled=True)
        gram = lax.psum(local_gram(sampled), "row") / M
        outputs.append(make_basis(rows_here, gram))
    return jnp.stack(outputs, axis=0)


def solution(mesh):
    return jax.shard_map(
        body,
        mesh=mesh,
        in_specs=(P(None, "row", "col"), P(None, "row", "col"), P("col", None)),
        out_specs=P(None, ("row", "col"), None),
        check_vma=False,
    )
```

profile of v0, /device:TPU:1, one launch (start us, length us, event | category | flops | bytes accessed | tf_op | source)
XLA Modules:
  0.0 823.3 jit_solution(7290686633852218556)
XLA Ops:
  6.5 0.8 subtract_convert_fusion.1
  7.3 1.4 fusion.70
  9.1 1.8 fusion.4
  11.4 1.8 fusion.2
  13.3 91.7 %reduce-scatter.3.cloned.1.call-done = f32[48,512]{1,0:T(8,128)} async-done(((f32[768,512]{1,0:T(8,128)}), f32[48,512]{1,0:T(8,128)}) %reduce-scatter.3.cloned.1.call-update) | async-done | bytes 98320 | tf_op jit(solution)/shard_map/reduce_scatter | solution.py:40
  105.0 93.3 %reduce-scatter.5.cloned.1.call-done = f32[48,512]{1,0:T(8,128)} async-done(((f32[768,512]{1,0:T(8,128)}), f32[48,512]{1,0:T(8,128)}) %reduce-scatter.5.cloned.1.call-update) | async-done | bytes 98320 | tf_op jit(solution)/shard_map/reduce_scatter | solution.py:40
  198.4 61.8 %all-gather.3.cloned.1.call-done = f32[768,512]{1,0:T(8,128)} async-done(((f32[48,512]{1,0:T(8,128)}), f32[768,512]{1,0:T(8,128)}) %all-gather.3.cloned.1.call-update) | async-done | bytes 1572880 | tf_op jit(solution)/shard_map/all_gather | solution.py:46
  260.2 5.6 fusion.71
  265.8 55.8 %all-gather.5.cloned.1.call-done = f32[768,512]{1,0:T(8,128)} async-done(((f32[48,512]{1,0:T(8,128)}), f32[768,512]{1,0:T(8,128)}) %all-gather.5.cloned.1.call-update) | async-done | bytes 1572880 | tf_op jit(solution)/shard_map/all_gather | solution.py:46
  321.6 5.6 fusion.72
  327.2 217.0 %all-reduce.4.cloned.1.call-done = (f32[512,512]{0,1:T(8,128)}, f32[512,512]{0,1:T(8,128)}) async-done(((f32[512,512]{0,1:T(8,128)}, f32[512,512]{0,1:T(8,128)}), (f32[512,512]{0,1:T(8,128)}, f32[512,512]{0,1:T(8,128)})) %all-reduce.4.cloned.1.call-update) | async-done | bytes 2097168 | tf_op jit(solution)/shard_map/psum | solution.py:47
  544.2 1.3 broadcast_multiply_fusion.1
  545.9 0.9 copy-done.2
  547.1 11.7 %cholesky.286 = f32[128,128]{1,0:T(8,128)S(1)} custom-call(f32[128,128]{1,0:T(8,128)S(1)} %cholesky.426), custom_call_target="Cholesky" | custom-call | tf_op jit(solution)/shard_map/jit(cholesky)/cholesky | solution.py:12
  558.8 10.0 %custom-call.27 = f32[1,128,128]{1,2,0:T(8,128)S(1)} custom-call(f32[1,128,128]{2,1,0:T(8,128)S(1)} %get-tuple-element.56), custom_call_target="InvertDiagBlocksLowerTriangular" | custom-call | tf_op jit(solution)/shard_map/jit(cholesky)/cholesky | solution.py:12
  569.6 11.7 %cholesky.305 = f32[128,128]{1,0:T(8,128)S(1)} custom-call(f32[128,128]{1,0:T(8,128)S(1)} %cholesky.430), custom_call_target="Cholesky" | custom-call | tf_op jit(solution)/shard_map/jit(cholesky)/cholesky | solution.py:12
  581.4 0.6 compare_reduce_fusion.6
  582.0 0.7 compare_reduce_fusion.7
  582.7 9.8 %custom-call.28 = f32[1,128,128]{1,2,0:T(8,128)S(1)} custom-call(f32[1,128,128]{2,1,0:T(8,128)S(1)} %get-tuple-element.53), custom_call_target="InvertDiagBlocksLowerTriangular" | custom-call | tf_op jit(solution)/shard_map/jit(cholesky)/cholesky | solution.py:12
  593.2 11.7 %cholesky.326 = f32[128,128]{1,0:T(8,128)S(1)} custom-call(f32[128,128]{1,0:T(8,128)S(1)} %cholesky.435), custom_call_target="Cholesky" | custom-call | tf_op jit(solution)/shard_map/jit(cholesky)/cholesky | solution.py:12
  605.0 0.7 compare_reduce_fusion.5
  605.6 10.2 %custom-call.29 = f32[1,128,128]{1,2,0:T(8,128)S(1)} custom-call(f32[1,128,128]{2,1,0:T(8,128)S(1)} %get-tuple-element.50), custom_call_target="InvertDiagBlocksLowerTriangular" | custom-call | tf_op jit(solution)/shard_map/jit(cholesky)/cholesky | solution.py:12
  616.4 11.7 %cholesky.343 = f32[128,128]{1,0:T(8,128)S(1)} custom-call(f32[128,128]{1,0:T(8,128)S(1)} %convolution_subtract_fusion.5), custom_call_target="Cholesky" | custom-call | tf_op jit(solution)/shard_map/jit(cholesky)/cholesky | solution.py:12
  628.2 0.7 compare_reduce_fusion.4
  631.6 8.1 while.4
  632.3 1.3 bitcast_dynamic-update-slice_fusion.4
  634.3 1.3 bitcast_dynamic-update-slice_fusion.4
  636.3 1.3 bitcast_dynamic-update-slice_fusion.4
  638.4 1.3 bitcast_dynamic-update-slice_fusion.4
  639.7 39.5 %custom-call.30 = f32[4,128,128]{1,2,0:T(8,128)S(1)} custom-call(f32[4,128,128]{2,1,0:T(8,128)S(1)} %get-tuple-element.21), custom_call_target="InvertDiagBlocksLowerTriangular" | custom-call | tf_op jit(solution)/shard_map/triangular_solve/custom-call.3 | solution.py:13
  680.8 0.7 fusion.24
  682.2 11.7 %cholesky.358 = f32[128,128]{1,0:T(8,128)S(1)} custom-call(f32[128,128]{1,0:T(8,128)S(1)} %cholesky.439), custom_call_target="Cholesky" | custom-call | tf_op jit(solution)/shard_map/jit(cholesky)/cholesky | solution.py:12
  693.9 9.8 %custom-call.31 = f32[1,128,128]{1,2,0:T(8,128)S(1)} custom-call(f32[1,128,128]{2,1,0:T(8,128)S(1)} %get-tuple-element.66), custom_call_target="InvertDiagBlocksLowerTriangular" | custom-call | tf_op jit(solution)/shard_map/jit(cholesky)/cholesky | solution.py:12
  704.5 11.7 %cholesky.377 = f32[128,128]{1,0:T(8,128)S(1)} custom-call(f32[128,128]{1,0:T(8,128)S(1)} %cholesky.443), custom_call_target="Cholesky" | custom-call | tf_op jit(solution)/shard_map/jit(cholesky)/cholesky | solution.py:12
  716.9 0.7 compare_reduce_fusion.3
  717.6 10.0 %custom-call.32 = f32[1,128,128]{1,2,0:T(8,128)S(1)} custom-call(f32[1,128,128]{2,1,0:T(8,128)S(1)} %get-tuple-element.63), custom_call_target="InvertDiagBlocksLowerTriangular" | custom-call | tf_op jit(solution)/shard_map/jit(cholesky)/cholesky | solution.py:12
  728.3 11.7 %cholesky.398 = f32[128,128]{1,0:T(8,128)S(1)} custom-call(f32[128,128]{1,0:T(8,128)S(1)} %cholesky.448), custom_call_target="Cholesky" | custom-call | tf_op jit(solution)/shard_map/jit(cholesky)/cholesky | solution.py:12
  740.1 0.7 compare_reduce_fusion.1
  740.7 9.8 %custom-call.33 = f32[1,128,128]{1,2,0:T(8,128)S(1)} custom-call(f32[1,128,128]{2,1,0:T(8,128)S(1)} %get-tuple-element.60), custom_call_target="InvertDiagBlocksLowerTriangular" | custom-call | tf_op jit(solution)/shard_map/jit(cholesky)/cholesky | solution.py:12
  751.1 12.0 %cholesky.415 = f32[128,128]{1,0:T(8,128)S(1)} custom-call(f32[128,128]{1,0:T(8,128)S(1)} %convolution_subtract_fusion.4), custom_call_target="Cholesky" | custom-call | tf_op jit(solution)/shard_map/jit(cholesky)/cholesky | solution.py:12
  763.1 0.7 compare_reduce_fusion
  766.5 8.1 while.5
  767.2 1.3 bitcast_dynamic-update-slice_fusion.5
  769.3 1.3 bitcast_dynamic-update-slice_fusion.5
  771.3 1.3 bitcast_dynamic-update-slice_fusion.5
  773.3 1.3 bitcast_dynamic-update-slice_fusion.5
  774.7 39.3 %custom-call.34 = f32[4,128,128]{1,2,0:T(8,128)S(1)} custom-call(f32[4,128,128]{2,1,0:T(8,128)S(1)} %get-tuple-element.22), custom_call_target="InvertDiagBlocksLowerTriangular" | custom-call | tf_op jit(solution)/shard_map/triangular_solve/custom-call.3 | solution.py:13
  815.6 0.7 pad_maximum_fusion
  (97 shorter events, 16.1 us)
Async XLA Ops:
  6.5 2.6 copy-start
  6.5 98.4 %reduce-scatter.3.cloned.1.call-start = ((), (), s32[]{:S(2)}) async-start(), calls=%async_computation.2 | async-start | bytes 1671168 | tf_op jit(solution)/shard_map/reduce_scatter | solution.py:40
  10.9 187.4 %reduce-scatter.5.cloned.1.call-start = ((), (), s32[]{:S(2)}) async-start(), calls=%async_computation.4 | async-start | bytes 1671168 | tf_op jit(solution)/shard_map/reduce_scatter | solution.py:40
  13.2 247.0 %all-gather.3.cloned.1.call-start = ((), (), s32[]{:S(2)}) async-start(), calls=%async_computation.3 | async-start | bytes 1671168 | tf_op jit(solution)/shard_map/all_gather | solution.py:46
  104.9 216.6 %all-gather.5.cloned.1.call-start = ((), (), s32[]{:S(2)}) async-start(), calls=%async_computation.5 | async-start | bytes 1671168 | tf_op jit(solution)/shard_map/all_gather | solution.py:46
  198.4 345.9 %all-reduce.4.cloned.1.call-start = ((), (), s32[]{:S(2)}) async-start(), calls=%async_computation.6 | async-start | bytes 4194304 | tf_op jit(solution)/shard_map/psum | solution.py:47
  545.6 1.2 copy-start.2
  631.4 47.8 %copy-start.4 = (f32[48,512]{1,0:T(8,128)S(1)}, f32[48,512]{1,0:T(8,128)}, u32[]{:S(2)}) copy-start(f32[48,512]{1,0:T(8,128)} %reduce-scatter.3.cloned.1.call-done) | copy-start | bytes 294916
  631.5 49.9 %copy-start.1 = (f32[512,512]{0,1:T(8,128)S(1)}, f32[512,512]{0,1:T(8,128)}, u32[]{:S(2)}) copy-start(f32[512,512]{0,1:T(8,128)} %get-tuple-element.39) | copy-start | bytes 3145732
  766.4 47.7 %copy-start.3 = (f32[48,512]{1,0:T(8,128)S(1)}, f32[48,512]{1,0:T(8,128)}, u32[]{:S(2)}) copy-start(f32[48,512]{1,0:T(8,128)} %reduce-scatter.5.cloned.1.call-done) | copy-start | bytes 294916
  766.5 49.1 %copy-start.5 = (f32[1,48,512]{2,1,0:T(8,128)S(1)}, f32[1,48,512]{2,1,0:T(8,128)}, u32[]{:S(2)}) copy-start(f32[1,48,512]{2,1,0:T(8,128)} %fusion.24) | copy-start | bytes 294916
Sparse Core Ops, SparseCore 0:
  11.4 93.4 reduce-scatter.2
  109.0 89.2 reduce-scatter.4
  201.4 58.8 all-gather.2
  263.1 58.4 all-gather.4
  327.3 216.8 all-reduce.3
where the time goes:
time: 833 us; the launch traced here: 823 us
  waiting for transfers between devices  520 us (62%)
  other arithmetic  242 us (29%)
  matrix products  21.5 us (3%)
  local copies, waits for them, and re-layouts  20.2 us (2%)
  between operations  19.1 us (2%)
    psum x1, waiting for transfers between devices, body(): gram = lax.psum(local_gram(sampled), 'row') / M  217 us
    reduce_scatter x2, waiting for transfers between devices, body(): lax.psum_scatter(jnp.dot(leftover, sketch, preferred_element_type=jnp.flo...  185 us
    another operation x30, other arithmetic, make_basis(): lower = jnp.linalg.cholesky(gram)  159 us
    all_gather x2, waiting for transfers between devices, body(): sampled = lax.all_gather(rows_here, 'col', axis=0, tiled=True)  118 us
    another operation x5, other arithmetic, make_basis(): lax.linalg.triangular_solve(lower, rows_here, left_side=False, lower=True...  79.1 us
  transfers between devices with their start and end apart: 5, of which 5 were waited for; matrix products, arithmetic and copies ran while one was open for 1% of the time, Pallas kernels for 0%

commit v1 on v0

--- a/solution.py
+++ b/solution.py
@@ -43,7 +43,9 @@
             scatter_dimension=0,
             tiled=True,
         )
-        sampled = lax.all_gather(rows_here, "col", axis=0, tiled=True)
+        sampled = jnp.concatenate(
+            lax.all_to_all(jnp.stack([rows_here] * lax.axis_size("col")), "col", 0, 0), axis=0
+        )
         gram = lax.psum(local_gram(sampled), "row") / M
         outputs.append(make_basis(rows_here, gram))
     return jnp.stack(outputs, axis=0)

time: 833 us -> 730 us (0.88)
  waiting for transfers between devices: 520 us -> 414 us
  starting transfers between devices: 0.16 us -> 9.03 us
    all_gather x2 -> x0, waiting for transfers between devices: 118 us -> none  [body(): sampled = lax.all_gather(rows_here, 'col', axis=0, tiled=True)]
    all_to_all x0 -> x2, waiting for transfers between devices: none -> 15.9 us  [body(): lax.all_to_all(jnp.stack([rows_here] * lax.axis_size('col')), 'col', 0, 0)]
    all_to_all x0 -> x2, starting transfers between devices: none -> 8.77 us  [body(): lax.all_to_all(jnp.stack([rows_here] * lax.axis_size('col')), 'col', 0, 0)]
  transfers between devices with their start and end apart: 5 -> 5, of which waited for: 5 -> 4; matrix products, arithmetic and copies ran while one was open for 1% -> 1% of each run, Pallas kernels for 0% -> 0%
where the time goes in v1:
time: 730 us; the launch traced here: 727 us
  waiting for transfers between devices  414 us (57%)
  other arithmetic  242 us (33%)
  local copies, waits for them, and re-layouts  24.7 us (3%)
  between operations  19 us (3%)
  matrix products  17.8 us (2%)
  starting transfers between devices  9.03 us (1%)
    psum x1, waiting for transfers between devices, body(): gram = lax.psum(local_gram(sampled), 'row') / M  218 us
    reduce_scatter x2, waiting for transfers between devices, body(): lax.psum_scatter(jnp.dot(leftover, sketch, preferred_element_type=jnp.flo...  180 us
    another operation x30, other arithmetic, make_basis(): lower = jnp.linalg.cholesky(gram)  159 us
    another operation x5, other arithmetic, make_basis(): lax.linalg.triangular_solve(lower, rows_here, left_side=False, lower=True...  79.1 us
    another operation x27, local copies, waits for them, and re-layouts, make_basis(): lax.linalg.triangular_solve(lower, rows_here, left_side=False, lower=True...  16.2 us
    all_to_all x2, waiting for transfers between devices, body(): lax.all_to_all(jnp.stack([rows_here] * lax.axis_size('col')), 'col', 0, 0)  15.9 us
  transfers between devices with their start and end apart: 5, of which 4 were waited for; matrix products, arithmetic and copies ran while one was open for 1% of the time, Pallas kernels for 0%

profile of v1, /device:TPU:1, one launch (start us, length us, event | category | flops | bytes accessed | tf_op | source)
XLA Modules:
  0.0 727.3 jit_solution(9606499625010721038)
XLA Ops:
  6.5 0.8 subtract_convert_fusion.1
  7.3 1.4 fusion.70
  9.1 1.8 fusion.2
  11.4 1.8 fusion.4
  13.2 91.7 %reduce-scatter.5.cloned.1.call-done = f32[48,512]{1,0:T(8,128)} async-done(((f32[768,512]{1,0:T(8,128)}), f32[48,512]{1,0:T(8,128)}) %reduce-scatter.5.cloned.1.call-update) | async-done | bytes 98320 | tf_op jit(solution)/shard_map/reduce_scatter | solution.py:40
  105.0 2.3 stack.12
  107.2 4.4 all-to-all-start.1
  111.6 88.6 %reduce-scatter.3.cloned.1.call-done = f32[48,512]{1,0:T(8,128)} async-done(((f32[768,512]{1,0:T(8,128)}), f32[48,512]{1,0:T(8,128)}) %reduce-scatter.3.cloned.1.call-update) | async-done | bytes 98320 | tf_op jit(solution)/shard_map/reduce_scatter | solution.py:40
  200.2 2.2 stack.10
  202.4 4.4 all-to-all-start
  207.0 3.7 convolution_bitcast_fusion
  210.8 15.9 %all-to-all-done = f32[16,48,512]{2,1,0:T(8,128)S(1)} async-done(((f32[16,48,512]{2,1,0:T(8,128)}), f32[16,48,512]{2,1,0:T(8,128)S(1)}, u32[]{:S(2)}, u32[]{:S(2)}) %all-to-all-start) | async-done | bytes 1572896 | tf_op jit(solution)/shard_map/all_to_all | solution.py:47
  226.7 3.7 convolution_bitcast_fusion.1
  230.4 217.9 %all-reduce.4.cloned.1.call-done = (f32[512,512]{0,1:T(8,128)}, f32[512,512]{0,1:T(8,128)}) async-done(((f32[512,512]{0,1:T(8,128)}, f32[512,512]{0,1:T(8,128)}), (f32[512,512]{0,1:T(8,128)}, f32[512,512]{0,1:T(8,128)})) %all-reduce.4.cloned.1.call-update) | async-done | bytes 2097168 | tf_op jit(solution)/shard_map/psum | solution.py:49
  448.3 1.3 broadcast_multiply_fusion.1
  449.9 0.9 copy-done.2
  451.1 11.7 %cholesky.286 = f32[128,128]{1,0:T(8,128)S(1)} custom-call(f32[128,128]{1,0:T(8,128)S(1)} %cholesky.426), custom_call_target="Cholesky" | custom-call | tf_op jit(solution)/shard_map/jit(cholesky)/cholesky | solution.py:12
  462.8 10.0 %custom-call.27 = f32[1,128,128]{1,2,0:T(8,128)S(1)} custom-call(f32[1,128,128]{2,1,0:T(8,128)S(1)} %get-tuple-element.56), custom_call_target="InvertDiagBlocksLowerTriangular" | custom-call | tf_op jit(solution)/shard_map/jit(cholesky)/cholesky | solution.py:12
  473.6 11.7 %cholesky.305 = f32[128,128]{1,0:T(8,128)S(1)} custom-call(f32[128,128]{1,0:T(8,128)S(1)} %cholesky.430), custom_call_target="Cholesky" | custom-call | tf_op jit(solution)/shard_map/jit(cholesky)/cholesky | solution.py:12
  486.0 0.7 compare_reduce_fusion.7
  486.7 9.8 %custom-call.28 = f32[1,128,128]{1,2,0:T(8,128)S(1)} custom-call(f32[1,128,128]{2,1,0:T(8,128)S(1)} %get-tuple-element.53), custom_call_target="InvertDiagBlocksLowerTriangular" | custom-call | tf_op jit(solution)/shard_map/jit(cholesky)/cholesky | solution.py:12
  497.2 11.7 %cholesky.326 = f32[128,128]{1,0:T(8,128)S(1)} custom-call(f32[128,128]{1,0:T(8,128)S(1)} %cholesky.435), custom_call_target="Cholesky" | custom-call | tf_op jit(solution)/shard_map/jit(cholesky)/cholesky | solution.py:12
  508.9 0.7 compare_reduce_fusion.5
  509.7 10.2 %custom-call.29 = f32[1,128,128]{1,2,0:T(8,128)S(1)} custom-call(f32[1,128,128]{2,1,0:T(8,128)S(1)} %get-tuple-element.50), custom_call_target="InvertDiagBlocksLowerTriangular" | custom-call | tf_op jit(solution)/shard_map/jit(cholesky)/cholesky | solution.py:12
  520.5 11.7 %cholesky.343 = f32[128,128]{1,0:T(8,128)S(1)} custom-call(f32[128,128]{1,0:T(8,128)S(1)} %convolution_subtract_fusion.5), custom_call_target="Cholesky" | custom-call | tf_op jit(solution)/shard_map/jit(cholesky)/cholesky | solution.py:12
  535.6 8.2 %while.4 = (s32[]{:T(128)}, f32[512,512]{1,0:T(8,128)S(1)}, s32[4,2]{0,1:T(2,128)S(1)}, f32[4,128,128]{2,1,0:T(8,128)S(1)}, s32[]{:T(128)}) while((s32[]{:T(128)}, f32[512,512]{1,0:T(8,128)S(1)}, s32[4,2]{0,1:T(2,128)S(1)}, f32[4,128,128]{2,1,0:T(8,128)S(1)}, s32[]{:T(128)}) %tuple.56), condition=%wide.while_cond, body=%wide.while_body.sunk | while | flops 2 | bytes 131181 | solution.py:13
  536.3 1.3 bitcast_dynamic-update-slice_fusion.4
  538.4 1.3 bitcast_dynamic-update-slice_fusion.4
  540.4 1.3 bitcast_dynamic-update-slice_fusion.4
  542.4 1.3 bitcast_dynamic-update-slice_fusion.4
  543.8 39.5 %custom-call.30 = f32[4,128,128]{1,2,0:T(8,128)S(1)} custom-call(f32[4,128,128]{2,1,0:T(8,128)S(1)} %get-tuple-element.21), custom_call_target="InvertDiagBlocksLowerTriangular" | custom-call | tf_op jit(solution)/shard_map/triangular_solve/custom-call.3 | solution.py:13
  586.3 11.7 %cholesky.358 = f32[128,128]{1,0:T(8,128)S(1)} custom-call(f32[128,128]{1,0:T(8,128)S(1)} %cholesky.439), custom_call_target="Cholesky" | custom-call | tf_op jit(solution)/shard_map/jit(cholesky)/cholesky | solution.py:12
  598.0 9.8 %custom-call.31 = f32[1,128,128]{1,2,0:T(8,128)S(1)} custom-call(f32[1,128,128]{2,1,0:T(8,128)S(1)} %get-tuple-element.66), custom_call_target="InvertDiagBlocksLowerTriangular" | custom-call | tf_op jit(solution)/shard_map/jit(cholesky)/cholesky | solution.py:12
  608.6 11.7 %cholesky.377 = f32[128,128]{1,0:T(8,128)S(1)} custom-call(f32[128,128]{1,0:T(8,128)S(1)} %cholesky.443), custom_call_target="Cholesky" | custom-call | tf_op jit(solution)/shard_map/jit(cholesky)/cholesky | solution.py:12
  621.0 0.7 compare_reduce_fusion.3
  621.7 10.0 %custom-call.32 = f32[1,128,128]{1,2,0:T(8,128)S(1)} custom-call(f32[1,128,128]{2,1,0:T(8,128)S(1)} %get-tuple-element.63), custom_call_target="InvertDiagBlocksLowerTriangular" | custom-call | tf_op jit(solution)/shard_map/jit(cholesky)/cholesky | solution.py:12
  632.4 11.7 %cholesky.398 = f32[128,128]{1,0:T(8,128)S(1)} custom-call(f32[128,128]{1,0:T(8,128)S(1)} %cholesky.448), custom_call_target="Cholesky" | custom-call | tf_op jit(solution)/shard_map/jit(cholesky)/cholesky | solution.py:12
  644.1 0.7 compare_reduce_fusion.1
  644.9 9.8 %custom-call.33 = f32[1,128,128]{1,2,0:T(8,128)S(1)} custom-call(f32[1,128,128]{2,1,0:T(8,128)S(1)} %get-tuple-element.60), custom_call_target="InvertDiagBlocksLowerTriangular" | custom-call | tf_op jit(solution)/shard_map/jit(cholesky)/cholesky | solution.py:12
  655.3 12.0 %cholesky.415 = f32[128,128]{1,0:T(8,128)S(1)} custom-call(f32[128,128]{1,0:T(8,128)S(1)} %convolution_subtract_fusion.4), custom_call_target="Cholesky" | custom-call | tf_op jit(solution)/shard_map/jit(cholesky)/cholesky | solution.py:12
  667.3 0.7 compare_reduce_fusion
  670.7 8.1 %while.5 = (s32[]{:T(128)}, f32[512,512]{1,0:T(8,128)S(1)}, s32[4,2]{0,1:T(2,128)S(1)}, f32[4,128,128]{2,1,0:T(8,128)S(1)}, s32[]{:T(128)}) while((s32[]{:T(128)}, f32[512,512]{1,0:T(8,128)S(1)}, s32[4,2]{0,1:T(2,128)S(1)}, f32[4,128,128]{2,1,0:T(8,128)S(1)}, s32[]{:T(128)}) %tuple.66), condition=%wide.while_cond.clone, body=%wide.while_body.clone.sunk | while | flops 2 | bytes 131181 | solution.py:13
  671.4 1.3 bitcast_dynamic-update-slice_fusion.5
  673.4 1.3 bitcast_dynamic-update-slice_fusion.5
  675.5 1.3 bitcast_dynamic-update-slice_fusion.5
  677.5 1.3 bitcast_dynamic-update-slice_fusion.5
  678.9 39.3 %custom-call.34 = f32[4,128,128]{1,2,0:T(8,128)S(1)} custom-call(f32[4,128,128]{2,1,0:T(8,128)S(1)} %get-tuple-element.22), custom_call_target="InvertDiagBlocksLowerTriangular" | custom-call | tf_op jit(solution)/shard_map/triangular_solve/custom-call.3 | solution.py:13
  719.8 0.7 pad_maximum_fusion
  (97 shorter events, 18.1 us)
Async XLA Ops:
  6.5 2.6 copy-start
  6.5 98.4 %reduce-scatter.5.cloned.1.call-start = ((), (), s32[]{:S(2)}) async-start(), calls=%async_computation.5 | async-start | bytes 1671168 | tf_op jit(solution)/shard_map/reduce_scatter | solution.py:40
  10.9 189.2 %reduce-scatter.3.cloned.1.call-start = ((), (), s32[]{:S(2)}) async-start(), calls=%async_computation.4 | async-start | bytes 1671168 | tf_op jit(solution)/shard_map/reduce_scatter | solution.py:40
  107.2 93.0 %all-to-all-start.1 = ((f32[16,48,512]{2,1,0:T(8,128)}), f32[16,48,512]{2,1,0:T(8,128)S(1)}, u32[]{:S(2)}, u32[]{:S(2)}) async-start(f32[16,48,512]{2,1,0:T(8,128)} %stack.12), calls=%async_computation.3 | async-start | bytes 3145728 | tf_op jit(solution)/shard_map/all_to_all | solution.py:47
  202.4 24.2 %all-to-all-start = ((f32[16,48,512]{2,1,0:T(8,128)}), f32[16,48,512]{2,1,0:T(8,128)S(1)}, u32[]{:S(2)}, u32[]{:S(2)}) async-start(f32[16,48,512]{2,1,0:T(8,128)} %stack.10), calls=%async_computation.1 | async-start | bytes 3145728 | tf_op jit(solution)/shard_map/all_to_all | solution.py:47
  206.8 241.4 %all-reduce.4.cloned.1.call-start = ((), (), s32[]{:S(2)}) async-start(), calls=%async_computation.6 | async-start | bytes 4194304 | tf_op jit(solution)/shard_map/psum | solution.py:49
  449.6 1.2 copy-start.2
  535.5 47.9 %copy-start.4 = (f32[48,512]{1,0:T(8,128)S(1)}, f32[48,512]{1,0:T(8,128)}, u32[]{:S(2)}) copy-start(f32[48,512]{1,0:T(8,128)} %reduce-scatter.3.cloned.1.call-done) | copy-start | bytes 294916
  535.6 49.9 %copy-start.1 = (f32[512,512]{0,1:T(8,128)S(1)}, f32[512,512]{0,1:T(8,128)}, u32[]{:S(2)}) copy-start(f32[512,512]{0,1:T(8,128)} %get-tuple-element.39) | copy-start | bytes 3145732
  670.5 47.7 %copy-start.3 = (f32[48,512]{1,0:T(8,128)S(1)}, f32[48,512]{1,0:T(8,128)}, u32[]{:S(2)}) copy-start(f32[48,512]{1,0:T(8,128)} %reduce-scatter.5.cloned.1.call-done) | copy-start | bytes 294916
  670.7 49.1 %copy-start.5 = (f32[1,48,512]{2,1,0:T(8,128)S(1)}, f32[1,48,512]{2,1,0:T(8,128)}, u32[]{:S(2)}) copy-start(f32[1,48,512]{2,1,0:T(8,128)} %fusion.24) | copy-start | bytes 294916
Sparse Core Ops, SparseCore 0:
  11.4 93.4 reduce-scatter.4
  109.0 91.1 reduce-scatter.2
  230.5 217.7 all-reduce.3
